TPU v7x, 512 devices: a whole 4x8x8 slice. The times are simulated.
512 devices in a mesh: dp: 16 (over x_lo, y), tensor: 32 (over x_hi, z, core).
Axes of the slice: x: 4 (x_hi: 2, x_lo: 2; x = x_hi * 2 + x_lo), y: 8, z: 8, core: 2. Of those that a mesh axis runs over, the one named last changes fastest.
Arguments:
- tokens: bfloat16 [4096, 14336], P('dp', 'tensor'), may hold values from -6 to 6
- base_weight: bfloat16 [14336, 4096], P('tensor'), may hold values from -0.5 to 0.5
- adapter_down: bfloat16 [16, 14336, 16], P(None, 'tensor'), may hold values from -0.046875 to 0.046875
- adapter_up: bfloat16 [16, 16, 4096], P(None, None, 'tensor'), may hold values from -1.5 to 1.5
- magnitude: bfloat16 [16, 4096], P(None, 'tensor'), may hold values from 0.5 to 2
- seg_lengths: int32 [16], replicated, may hold values from 1 to 2048, 4096 in all
- cotangent: bfloat16 [4096, 4096], P('dp', 'tensor'), may hold values from -6 to 6
Outputs:
- projected: bfloat16 [4096, 4096], P('dp', 'tensor')
- grad_tokens: bfloat16 [4096, 14336], P('dp', 'tensor')
- grad_down: bfloat16 [16, 14336, 16], P(None, 'tensor')
- grad_up: float32 [16, 16, 4096], P(None, None, 'tensor')
- grad_magnitude: float32 [16, 4096], P(None, 'tensor')
Inputs may be any that keep to these rules, and one draw needn't show every extreme that they name: The segments cover all 4096 tokens in order: seg_lengths sums to 4096.
All inputs are finite; a program needn't handle non-finite values.
Results may differ from a plain program's by a relative error of at most 0.019.
Values may be sent and summed in bfloat16 or wider, within the bound.
No kernel may reach another device: no remote copies, remote signals or barrier semaphores. Data moves between devices by JAX's collectives and lax.ppermute only.
A program may use at most 64 MiB of HBM per device.

v0:
```python
import jax
import jax.numpy as jnp
from jax import lax
from jax.sharding import PartitionSpec as P

HIGHEST_MODE = lax.Precision.HIGHEST
EPSILON = 1e-06


def from_everyone(shard, axis):
    size = lax.axis_size(axis)
    return lax.all_to_all(
        jnp.broadcast_to(shard[None], (size, *shard.shape)), axis, 0, 0, tiled=True
    )


def taken_together(shard, axis):
    return from_everyone(shard, axis).sum(axis=0)


def split_up(shard, dim, size):
    lengths = shard.shape
    tiles = shard.reshape(*lengths[:dim], size, lengths[dim] // size, *lengths[dim + 1 :])
    return jnp.moveaxis(tiles, dim, 0)


def summed_on_arrival(shard, axis, dim):
    size = lax.axis_size(axis)
    tiles = lax.all_to_all(split_up(shard, dim, size), axis, 0, 0, tiled=True)
    return jnp.sum(tiles.astype(jnp.float32), axis=0)


def padded_to(lines, size):
    spare = -lines.shape[0] % size
    if not spare:
        return lines
    return jnp.concatenate([lines, jnp.zeros((spare, *lines.shape[1:]), lines.dtype)])


def laid_out(tiles, dim):
    lengths = list(tiles.shape[1:])
    lengths[dim] *= tiles.shape[0]
    return jnp.moveaxis(tiles, 0, dim).reshape(lengths)


def collect(shard, axis, dim):
    return laid_out(from_everyone(shard, axis), dim)


def total_of(shard, axes):
    lines = shard.reshape(-1, shard.shape[-1])
    own = summed_on_arrival(padded_to(lines, lax.axis_size(axes)), axes, 0)
    whole = collect(own.astype(jnp.bfloat16), axes, 0)
    return whole[: len(lines)].reshape(shard.shape).astype(jnp.float32)


def member_table(seg_lengths, first_token, token_count):
    seg_ends = jnp.cumsum(seg_lengths)
    seg_starts = seg_ends - seg_lengths
    positions = first_token + jnp.arange(token_count, dtype=jnp.int32)[:, None]
    return ((positions >= seg_starts[None, :]) & (positions < seg_ends[None, :])).astype(
        jnp.float32
    )


def pick_rank(member, spread):
    token_count, adapter_count = member.shape
    return jnp.einsum(
        "ta,tar->tr", member, spread.reshape(token_count, adapter_count, -1), precision=HIGHEST_MODE
    )


def expand_rank(member, low_rounded):
    widened = member[:, :, None] * low_rounded.astype(jnp.float32)[:, None, :]
    return widened.reshape(member.shape[0], -1).astype(jnp.bfloat16)


def local(tokens, base_weight, adapter_down, adapter_up, magnitude, seg_lengths, cotangent):
    token_count, own_rows = tokens.shape
    adapter_count, _, rank_width = adapter_down.shape
    own_width = adapter_up.shape[2]
    full_width = base_weight.shape[1]
    member = member_table(seg_lengths, lax.axis_index("dp") * token_count, token_count)
    down_flat = jnp.transpose(adapter_down, (1, 0, 2)).reshape(own_rows, adapter_count * rank_width)
    up_whole = lax.all_gather(adapter_up, "tensor", axis=2, tiled=True)
    spread = jnp.dot(tokens, down_flat, preferred_element_type=jnp.float32)
    low_rank = taken_together(pick_rank(member, spread), "tensor")
    low_wide = expand_rank(member, low_rank.astype(jnp.bfloat16))
    cross_terms = lax.dot_general(
        down_flat, base_weight, (((0,), (0,)), ((), ())), preferred_element_type=jnp.float32
    )
    up_float = up_whole.astype(jnp.float32)
    gram_matrix = jnp.einsum(
        "afr,afs->ars", adapter_down, adapter_down, preferred_element_type=jnp.float32
    )
    column_squares = jnp.sum(jnp.square(base_weight.astype(jnp.float32)), axis=0)
    cross_sum = jnp.sum(
        cross_terms.reshape(adapter_count, rank_width, full_width) * up_float, axis=1
    )
    gram_sum = jnp.sum(
        up_float * jnp.einsum("ars,asd->ard", gram_matrix, up_float, precision=HIGHEST_MODE), axis=1
    )
    partial_squares = column_squares[None, :] + 2.0 * cross_sum + gram_sum
    base_terms = jnp.dot(tokens, base_weight, preferred_element_type=jnp.float32)
    col_norms = jnp.sqrt(
        summed_on_arrival(partial_squares.astype(jnp.bfloat16), "tensor", 1) + EPSILON
    )
    base_own = summed_on_arrival(base_terms.astype(jnp.bfloat16), "tensor", 1)
    up_own = adapter_up.reshape(adapter_count * rank_width, own_width)
    hidden = base_own + jnp.dot(low_wide, up_own, preferred_element_type=jnp.float32)
    col_scale = magnitude.astype(jnp.float32) / col_norms
    token_scale = jnp.dot(member, col_scale, precision=HIGHEST_MODE)
    projected = (hidden * token_scale).astype(jnp.bfloat16)
    grad_in = cotangent.astype(jnp.float32)
    grad_mag_part = jnp.dot(member.T, grad_in * hidden, precision=HIGHEST_MODE)
    grad_own = (grad_in * token_scale).astype(jnp.bfloat16)
    grad_up_part = jnp.dot(low_wide.T, grad_own, preferred_element_type=jnp.float32)
    grad_up_part = grad_up_part.reshape(adapter_count, rank_width, own_width)
    back_spread = lax.dot_general(
        grad_own, up_own, (((1,), (1,)), ((), ())), preferred_element_type=jnp.float32
    )
    back_rank = taken_together(pick_rank(member, back_spread), "tensor")
    back_wide = expand_rank(member, back_rank.astype(jnp.bfloat16))
    start_grad = lax.dot_general(
        back_wide, down_flat, (((1,), (1,)), ((), ())), preferred_element_type=jnp.float32
    )
    grad_base = start_grad + lax.dot_general(
        lax.all_gather(grad_own, "tensor", axis=1, tiled=True),
        base_weight,
        (((1,), (1,)), ((), ())),
        preferred_element_type=jnp.float32,
    )
    grad_tokens = grad_base.astype(jnp.bfloat16)
    grad_down_part = lax.dot_general(
        tokens, back_wide, (((0,), (0,)), ((), ())), preferred_element_type=jnp.float32
    )
    grad_down_part = jnp.transpose(
        grad_down_part.reshape(own_rows, adapter_count, rank_width), (1, 0, 2)
    )
    mag_summed, up_summed, down_summed = (
        total_of(grad_mag_part.astype(jnp.bfloat16), "dp"),
        total_of(grad_up_part.astype(jnp.bfloat16), "dp"),
        total_of(grad_down_part.astype(jnp.bfloat16), "dp"),
    )
    grad_magnitude = mag_summed / col_norms
    return (projected, grad_tokens, down_summed.astype(jnp.bfloat16), up_summed, grad_magnitude)


def solution(mesh):
    placed = (
        P("dp", "tensor"),
        P("tensor", None),
        P(None, "tensor", None),
        P(None, None, "tensor"),
        P(None, "tensor"),
        P(),
        P("dp", "tensor"),
    )
    return jax.shard_map(
        local,
        mesh=mesh,
        in_specs=placed,
        out_specs=(
            P("dp", "tensor"),
            P("dp", "tensor"),
            P(None, "tensor", None),
            P(None, None, "tensor"),
            P(None, "tensor"),
        ),
        check_vma=False,
    )
```

profile of v0, /device:TPU:8, one launch (start us, length us, event | category | flops | bytes accessed | tf_op | source)
XLA Modules:
  0.0 259.1 jit_solution(895637971586263253)
XLA Ops:
  9.6 1.2 fusion.9
  11.6 13.2 %all-to-all-start.1 = ((f32[32,256,16]{1,2,0:T(8,128)}), f32[32,256,16]{1,2,0:T(8,128)S(1)}, u32[]{:S(2)}, u32[]{:S(2)}) async-start(f32[32,256,16]{1,2,0:T(8,128)} %broadcast_in_dim.10), calls=%async_computation.1 | async-start | bytes 1048576 | tf_op jit(solution)/shard_map/all_to_all | solution.py:12
  24.8 3.5 %fusion.5 = bf16[32,32,8,128]{3,2,1,0:T(8,128)(2,1)S(1)} fusion(bf16[256,448]{0,1:T(8,128)(2,1)} %param.7, bf16[448,4096]{1,0:T(8,128)(2,1)} %param.8), kind=kOutput, calls=%fused_computation.9 | convolution fusion | flops 940572672 | bytes 5996544 | tf_op jit(solution)/shard_map/dot_general | solution.py:104
  28.2 1.9 copy.37
  30.1 15.0 %all-to-all-done.1 = f32[32,256,16]{1,2,0:T(8,128)S(1)} async-done(((f32[32,256,16]{1,2,0:T(8,128)}), f32[32,256,16]{1,2,0:T(8,128)S(1)}, u32[]{:S(2)}, u32[]{:S(2)}) %all-to-all-start.1) | async-done | bytes 524320 | tf_op jit(solution)/shard_map/all_to_all | solution.py:12
  45.1 4.0 %all-to-all-start = ((bf16[32,256,128]{2,1,0:T(8,128)(2,1)}), bf16[32,256,128]{2,1,0:T(8,128)(2,1)S(1)}, u32[]{:S(2)}, u32[]{:S(2)}) async-start(bf16[32,256,128]{2,1,0:T(8,128)(2,1)} %bitcast.86), calls=%async_computation | async-start | bytes 4194304 | tf_op jit(solution)/shard_map/all_to_all | solution.py:29
  49.4 2.8 %multiply_reduce_fusion = f32[4096]{0:T(1024)S(1)} fusion(bf16[448,4096]{1,0:T(8,128)(2,1)} %param.8), kind=kLoop, calls=%fused_computation | loop fusion | flops 5500928 | bytes 3686400 | tf_op jit(solution)/shard_map/reduce_sum | solution.py:96
  52.2 59.5 %all-gather.3.cloned.1.call-done = bf16[16,16,4096]{2,1,0:T(8,128)(2,1)} async-done(((bf16[16,16,128]{2,1,0:T(8,128)(2,1)}), bf16[16,16,4096]{2,1,0:T(8,128)(2,1)}) %all-gather.3.cloned.1.call-update) | async-done | bytes 2097168 | tf_op jit(solution)/shard_map/all_gather | solution.py:85
  111.8 4.7 %fusion.4 = f32[16,4096]{1,0:T(8,128)S(1)} fusion(f32[16,16,16]{2,1,0:T(8,128)S(1)} %fusion.40, bf16[16,16,4096]{2,1,0:T(8,128)(2,1)} %all-gather.3.cloned.1.call-done), kind=kOutput, calls=%fused_computation.8 | convolution fusion | flops 204406784 | bytes 2375680 | tf_op jit(solution)/shard_map/ars,asd->ard/dot_general | solution.py:101
  116.6 4.3 %fusion.1 = f32[16,4096]{1,0:T(8,128)S(1)} fusion(bf16[16,16,4096]{2,1,0:T(8,128)(2,1)} %all-gather.3.cloned.1.call-done, bf16[448,4096]{1,0:T(8,128)(2,1)} %param.8, bf16[16,448,16]{1,2,0:T(8,128)(2,1)S(1)} %copy-done), kind=kOutput, calls=%fused_computation.7 | convolution fusion | flops 942604288 | bytes 6258688 | tf_op jit(solution)/shard_map/dot_general | solution.py:89
  121.8 6.6 %all-to-all-start.2 = ((bf16[32,16,128]{2,1,0:T(8,128)(2,1)}), bf16[32,16,128]{2,1,0:T(8,128)(2,1)S(1)}, u32[]{:S(2)}, u32[]{:S(2)}) async-start(bf16[32,16,128]{2,1,0:T(8,128)(2,1)} %copy.21), calls=%async_computation.2 | async-start | bytes 262144 | tf_op jit(solution)/shard_map/all_to_all | solution.py:29
  128.9 11.3 %all-to-all-done.2 = bf16[32,16,128]{2,1,0:T(8,128)(2,1)S(1)} async-done(((bf16[32,16,128]{2,1,0:T(8,128)(2,1)}), bf16[32,16,128]{2,1,0:T(8,128)(2,1)S(1)}, u32[]{:S(2)}, u32[]{:S(2)}) %all-to-all-start.2) | async-done | bytes 131104 | tf_op jit(solution)/shard_map/all_to_all | solution.py:29
  140.3 1.0 fusion.19
  142.2 7.8 %all-to-all-start.8 = ((bf16[16,1,128]{2,1,0:T(2,128)(2,1)}), bf16[16,1,128]{2,1,0:T(2,128)(2,1)S(1)}, u32[]{:S(2)}, u32[]{:S(2)}) async-start(bf16[16,1,128]{2,1,0:T(2,128)(2,1)} %copy.23), calls=%async_computation.8 | async-start | bytes 16384 | tf_op jit(solution)/shard_map/all_to_all | solution.py:29
  150.0 1.0 fusion.10
  151.1 6.0 %all-to-all-done.8 = bf16[16,1,128]{2,1,0:T(2,128)(2,1)S(1)} async-done(((bf16[16,1,128]{2,1,0:T(2,128)(2,1)}), bf16[16,1,128]{2,1,0:T(2,128)(2,1)S(1)}, u32[]{:S(2)}, u32[]{:S(2)}) %all-to-all-start.8) | async-done | bytes 4128 | tf_op jit(solution)/shard_map/all_to_all | solution.py:29
  157.1 0.9 broadcast_in_dim.11
  157.9 3.9 %all-to-all-start.3 = ((f32[32,256,16]{1,2,0:T(8,128)}), f32[32,256,16]{1,2,0:T(8,128)S(1)}, u32[]{:S(2)}, u32[]{:S(2)}) async-start(f32[32,256,16]{1,2,0:T(8,128)} %broadcast_in_dim.11), calls=%async_computation.3 | async-start | bytes 1048576 | tf_op jit(solution)/shard_map/all_to_all | solution.py:12
  161.9 1.6 convolution_convert_fusion.2
  163.5 18.5 %all-to-all-done.3 = f32[32,256,16]{1,2,0:T(8,128)S(1)} async-done(((f32[32,256,16]{1,2,0:T(8,128)}), f32[32,256,16]{1,2,0:T(8,128)S(1)}, u32[]{:S(2)}, u32[]{:S(2)}) %all-to-all-start.3) | async-done | bytes 524320 | tf_op jit(solution)/shard_map/all_to_all | solution.py:12
  182.6 4.5 %all-to-all-start.9 = ((bf16[16,1,128]{2,1,0:T(2,128)(2,1)}), bf16[16,1,128]{2,1,0:T(2,128)(2,1)S(1)}, u32[]{:S(2)}, u32[]{:S(2)}) async-start(bf16[16,1,128]{2,1,0:T(2,128)(2,1)} %broadcast_in_dim.14), calls=%async_computation.9 | async-start | bytes 16384 | tf_op jit(solution)/shard_map/all_to_all | solution.py:12
  187.2 7.1 %all-to-all-done.9 = bf16[16,1,128]{2,1,0:T(2,128)(2,1)S(1)} async-done(((bf16[16,1,128]{2,1,0:T(2,128)(2,1)}), bf16[16,1,128]{2,1,0:T(2,128)(2,1)S(1)}, u32[]{:S(2)}, u32[]{:S(2)}) %all-to-all-start.9) | async-done | bytes 4128 | tf_op jit(solution)/shard_map/all_to_all | solution.py:12
  194.2 4.7 %all-to-all-start.6 = ((bf16[16,16,128]{2,1,0:T(8,128)(2,1)}), bf16[16,16,128]{2,1,0:T(8,128)(2,1)S(1)}, u32[]{:S(2)}, u32[]{:S(2)}) async-start(bf16[16,16,128]{2,1,0:T(8,128)(2,1)} %convolution_convert_fusion.2), calls=%async_computation.6 | async-start | bytes 131072 | tf_op jit(solution)/shard_map/all_to_all | solution.py:29
  200.1 6.5 %all-to-all-done.6 = bf16[16,16,128]{2,1,0:T(8,128)(2,1)S(1)} async-done(((bf16[16,16,128]{2,1,0:T(8,128)(2,1)}), bf16[16,16,128]{2,1,0:T(8,128)(2,1)S(1)}, u32[]{:S(2)}, u32[]{:S(2)}) %all-to-all-start.6) | async-done | bytes 65568 | tf_op jit(solution)/shard_map/all_to_all | solution.py:29
  206.6 4.4 %all-to-all-start.4 = ((bf16[16,448,16]{1,2,0:T(8,128)(2,1)}), bf16[16,448,16]{1,2,0:T(8,128)(2,1)S(1)}, u32[]{:S(2)}, u32[]{:S(2)}) async-start(bf16[16,448,16]{1,2,0:T(8,128)(2,1)} %bitcast.19), calls=%async_computation.4 | async-start | bytes 524288 | tf_op jit(solution)/shard_map/all_to_all | solution.py:29
  211.0 9.1 %all-to-all-done.4 = bf16[16,448,16]{1,2,0:T(8,128)(2,1)S(1)} async-done(((bf16[16,448,16]{1,2,0:T(8,128)(2,1)}), bf16[16,448,16]{1,2,0:T(8,128)(2,1)S(1)}, u32[]{:S(2)}, u32[]{:S(2)}) %all-to-all-start.4) | async-done | bytes 229408 | tf_op jit(solution)/shard_map/all_to_all | solution.py:29
  220.7 4.2 %all-to-all-start.7 = ((bf16[16,16,128]{2,1,0:T(8,128)(2,1)}), bf16[16,16,128]{2,1,0:T(8,128)(2,1)S(1)}, u32[]{:S(2)}, u32[]{:S(2)}) async-start(bf16[16,16,128]{2,1,0:T(8,128)(2,1)} %broadcast_in_dim.13), calls=%async_computation.7 | async-start | bytes 131072 | tf_op jit(solution)/shard_map/all_to_all | solution.py:12
  225.0 7.6 %all-to-all-done.7 = bf16[16,16,128]{2,1,0:T(8,128)(2,1)S(1)} async-done(((bf16[16,16,128]{2,1,0:T(8,128)(2,1)}), bf16[16,16,128]{2,1,0:T(8,128)(2,1)S(1)}, u32[]{:S(2)}, u32[]{:S(2)}) %all-to-all-start.7) | async-done | bytes 65568 | tf_op jit(solution)/shard_map/all_to_all | solution.py:12
  233.3 4.3 %all-to-all-start.5 = ((bf16[16,448,16]{1,2,0:T(8,128)(2,1)}), bf16[16,448,16]{1,2,0:T(8,128)(2,1)S(1)}, u32[]{:S(2)}, u32[]{:S(2)}) async-start(bf16[16,448,16]{1,2,0:T(8,128)(2,1)} %broadcast_in_dim.12), calls=%async_computation.5 | async-start | bytes 524288 | tf_op jit(solution)/shard_map/all_to_all | solution.py:12
  238.9 7.8 %all-to-all-done.5 = bf16[16,448,16]{1,2,0:T(8,128)(2,1)S(1)} async-done(((bf16[16,448,16]{1,2,0:T(8,128)(2,1)}), bf16[16,448,16]{1,2,0:T(8,128)(2,1)S(1)}, u32[]{:S(2)}, u32[]{:S(2)}) %all-to-all-start.5) | async-done | bytes 229408 | tf_op jit(solution)/shard_map/all_to_all | solution.py:12
  246.7 3.8 %fusion.41 = f32[256,448]{0,1:T(8,128)S(1)} fusion(bf16[256,4096]{1,0:T(8,128)(2,1)} %all-gather.5.cloned.1.call-done, bf16[448,4096]{1,0:T(8,128)(2,1)} %param.8), kind=kOutput, calls=%fused_computation.65 | convolution fusion | flops 939524096 | bytes 6225920 | tf_op jit(solution)/shard_map/dot_general | solution.py:127
  250.5 1.0 fusion.7
  (51 shorter events, 11.0 us)
Async XLA Ops:
  7.2 2.4 copy-start
  7.2 104.6 %all-gather.3.cloned.1.call-start = ((), (), s32[]{:S(2)}) async-start(), calls=%async_computation.10 | async-start | bytes 2162688 | tf_op jit(solution)/shard_map/all_gather | solution.py:85
  11.6 33.5 %all-to-all-start.1 = ((f32[32,256,16]{1,2,0:T(8,128)}), f32[32,256,16]{1,2,0:T(8,128)S(1)}, u32[]{:S(2)}, u32[]{:S(2)}) async-start(f32[32,256,16]{1,2,0:T(8,128)} %broadcast_in_dim.10), calls=%async_computation.1 | async-start | bytes 1048576 | tf_op jit(solution)/shard_map/all_to_all | solution.py:12
  45.1 76.6 %all-to-all-start = ((bf16[32,256,128]{2,1,0:T(8,128)(2,1)}), bf16[32,256,128]{2,1,0:T(8,128)(2,1)S(1)}, u32[]{:S(2)}, u32[]{:S(2)}) async-start(bf16[32,256,128]{2,1,0:T(8,128)(2,1)} %bitcast.86), calls=%async_computation | async-start | bytes 4194304 | tf_op jit(solution)/shard_map/all_to_all | solution.py:29
  120.9 7.8 %copy-start.3 = (bf16[16,16,128]{2,1,0:T(8,128)(2,1)S(1)}, bf16[16,16,128]{2,1,0:T(8,128)(2,1)}, u32[]{:S(2)}) copy-start(bf16[16,16,128]{2,1,0:T(8,128)(2,1)} %param.10) | copy-start | bytes 196612
  120.9 19.4 %copy-start.2 = (bf16[256,128]{1,0:T(8,128)(2,1)S(1)}, bf16[256,128]{1,0:T(8,128)(2,1)}, u32[]{:S(2)}) copy-start(bf16[256,128]{1,0:T(8,128)(2,1)} %param.13) | copy-start | bytes 196612
  120.9 19.4 %copy-start.4 = (bf16[16,128]{1,0:T(8,128)(2,1)S(1)}, bf16[16,128]{1,0:T(8,128)(2,1)}, u32[]{:S(2)}) copy-start(bf16[16,128]{1,0:T(8,128)(2,1)} %param.11) | copy-start | bytes 12292
  121.1 77.9 %copy-start.1 = (bf16[256,448]{0,1:T(8,128)(2,1)S(1)}, bf16[256,448]{0,1:T(8,128)(2,1)}, u32[]{:S(2)}) copy-start(bf16[256,448]{0,1:T(8,128)(2,1)} %param.7) | copy-start | bytes 688132
  121.8 18.5 %all-to-all-start.2 = ((bf16[32,16,128]{2,1,0:T(8,128)(2,1)}), bf16[32,16,128]{2,1,0:T(8,128)(2,1)S(1)}, u32[]{:S(2)}, u32[]{:S(2)}) async-start(bf16[32,16,128]{2,1,0:T(8,128)(2,1)} %copy.21), calls=%async_computation.2 | async-start | bytes 262144 | tf_op jit(solution)/shard_map/all_to_all | solution.py:29
  128.3 118.4 %all-gather.5.cloned.1.call-start = ((), (), s32[]{:S(2)}) async-start(), calls=%async_computation.11 | async-start | bytes 2162688 | tf_op jit(solution)/shard_map/all_gather | solution.py:128
  142.2 14.9 %all-to-all-start.8 = ((bf16[16,1,128]{2,1,0:T(2,128)(2,1)}), bf16[16,1,128]{2,1,0:T(2,128)(2,1)S(1)}, u32[]{:S(2)}, u32[]{:S(2)}) async-start(bf16[16,1,128]{2,1,0:T(2,128)(2,1)} %copy.23), calls=%async_computation.8 | async-start | bytes 16384 | tf_op jit(solution)/shard_map/all_to_all | solution.py:29
  157.9 24.1 %all-to-all-start.3 = ((f32[32,256,16]{1,2,0:T(8,128)}), f32[32,256,16]{1,2,0:T(8,128)S(1)}, u32[]{:S(2)}, u32[]{:S(2)}) async-start(f32[32,256,16]{1,2,0:T(8,128)} %broadcast_in_dim.11), calls=%async_computation.3 | async-start | bytes 1048576 | tf_op jit(solution)/shard_map/all_to_all | solution.py:12
  182.6 11.6 %all-to-all-start.9 = ((bf16[16,1,128]{2,1,0:T(2,128)(2,1)}), bf16[16,1,128]{2,1,0:T(2,128)(2,1)S(1)}, u32[]{:S(2)}, u32[]{:S(2)}) async-start(bf16[16,1,128]{2,1,0:T(2,128)(2,1)} %broadcast_in_dim.14), calls=%async_computation.9 | async-start | bytes 16384 | tf_op jit(solution)/shard_map/all_to_all | solution.py:12
  194.2 12.4 %all-to-all-start.6 = ((bf16[16,16,128]{2,1,0:T(8,128)(2,1)}), bf16[16,16,128]{2,1,0:T(8,128)(2,1)S(1)}, u32[]{:S(2)}, u32[]{:S(2)}) async-start(bf16[16,16,128]{2,1,0:T(8,128)(2,1)} %convolution_convert_fusion.2), calls=%async_computation.6 | async-start | bytes 131072 | tf_op jit(solution)/shard_map/all_to_all | solution.py:29
  206.6 13.5 %all-to-all-start.4 = ((bf16[16,448,16]{1,2,0:T(8,128)(2,1)}), bf16[16,448,16]{1,2,0:T(8,128)(2,1)S(1)}, u32[]{:S(2)}, u32[]{:S(2)}) async-start(bf16[16,448,16]{1,2,0:T(8,128)(2,1)} %bitcast.19), calls=%async_computation.4 | async-start | bytes 524288 | tf_op jit(solution)/shard_map/all_to_all | solution.py:29
  220.7 11.8 %all-to-all-start.7 = ((bf16[16,16,128]{2,1,0:T(8,128)(2,1)}), bf16[16,16,128]{2,1,0:T(8,128)(2,1)S(1)}, u32[]{:S(2)}, u32[]{:S(2)}) async-start(bf16[16,16,128]{2,1,0:T(8,128)(2,1)} %broadcast_in_dim.13), calls=%async_computation.7 | async-start | bytes 131072 | tf_op jit(solution)/shard_map/all_to_all | solution.py:12
  233.3 13.5 %all-to-all-start.5 = ((bf16[16,448,16]{1,2,0:T(8,128)(2,1)}), bf16[16,448,16]{1,2,0:T(8,128)(2,1)S(1)}, u32[]{:S(2)}, u32[]{:S(2)}) async-start(bf16[16,448,16]{1,2,0:T(8,128)(2,1)} %broadcast_in_dim.12), calls=%async_computation.5 | async-start | bytes 524288 | tf_op jit(solution)/shard_map/all_to_all | solution.py:12
Sparse Core Ops, SparseCore 0:
  11.1 100.6 all-gather.2
  141.5 80.5 all-gather.4
where the time goes:
time: 260 us; the launch traced here: 259 us
  waiting for transfers between devices  149 us (57%)
  starting transfers between devices  57.6 us (22%)
  matrix products  23 us (9%)
  between operations  14.3 us (6%)
  local copies, waits for them, and re-layouts  9.3 us (4%)
  other arithmetic  5.62 us (2%)
    all_gather x1, waiting for transfers between devices, local(): up_whole = lax.all_gather(adapter_up, 'tensor', axis=2, tiled=True)  59.5 us
    all_to_all x5, waiting for transfers between devices, from_everyone(): lax.all_to_all(jnp.broadcast_to(shard[None], (size, *shard.shape)), axis,...  55.9 us
    all_to_all x5, waiting for transfers between devices, summed_on_arrival(): tiles = lax.all_to_all(split_up(shard, dim, size), axis, 0, 0, tiled=True)  33 us
    all_to_all x5, starting transfers between devices, from_everyone(): lax.all_to_all(jnp.broadcast_to(shard[None], (size, *shard.shape)), axis,...  30.1 us
    all_to_all x5, starting transfers between devices, summed_on_arrival(): tiles = lax.all_to_all(split_up(shard, dim, size), axis, 0, 0, tiled=True)  27.5 us
  transfers between devices with their start and end apart: 12, of which 10 were waited for; matrix products, arithmetic and copies ran while one was open for 12% of the time, Pallas kernels for 0%

commit v1 on v0

--- a/solution.py
+++ b/solution.py
@@ -82,7 +82,10 @@
     full_width = base_weight.shape[1]
     member = member_table(seg_lengths, lax.axis_index("dp") * token_count, token_count)
     down_flat = jnp.transpose(adapter_down, (1, 0, 2)).reshape(own_rows, adapter_count * rank_width)
-    up_whole = lax.all_gather(adapter_up, "tensor", axis=2, tiled=True)
+    peers = lax.axis_size("tensor")
+    tiles_2 = jnp.stack([adapter_up for _ in range(peers)])
+    tiles_2 = lax.all_to_all(tiles_2, "tensor", split_axis=0, concat_axis=0)
+    up_whole = jnp.concatenate(tiles_2, axis=2)
     spread = jnp.dot(tokens, down_flat, preferred_element_type=jnp.float32)
     low_rank = taken_together(pick_rank(member, spread), "tensor")
     low_wide = expand_rank(member, low_rank.astype(jnp.bfloat16))

time: 260 us -> 295 us (1.13)
  blocking collectives: 0 us -> 32.9 us
  waiting for transfers between devices: 149 us -> 162 us
  starting transfers between devices: 57.6 us -> 46.8 us
  matrix products: 23 us -> 20 us
    all_gather x1 -> x0, waiting for transfers between devices: 59.5 us -> none  [local(): up_whole = lax.all_gather(adapter_up, 'tensor', axis=2, tiled=True)]
    all_to_all x0 -> x1, waiting for transfers between devices: none -> 46.6 us  [local(): tiles_2 = lax.all_to_all(tiles_2, 'tensor', split_axis=0, concat_axis=0)]
    all_to_all x5, waiting for transfers between devices: 33 us -> 73.8 us  [summed_on_arrival(): tiles = lax.all_to_all(split_up(shard, dim, size), axis, 0, 0, tiled=True)]
    all_to_all x0 -> x1, blocking collectives: none -> 32.9 us  [from_everyone(): lax.all_to_all(jnp.broadcast_to(shard[None], (size, *shard.shape)), axis,...]
    all_to_all x5 -> x4, waiting for transfers between devices: 55.9 us -> 41.8 us  [from_everyone(): lax.all_to_all(jnp.broadcast_to(shard[None], (size, *shard.shape)), axis,...]
    all_to_all x5 -> x4, starting transfers between devices: 30.1 us -> 16.9 us  [from_everyone(): lax.all_to_all(jnp.broadcast_to(shard[None], (size, *shard.shape)), axis,...]
    all_to_all x0 -> x1, starting transfers between devices: none -> 4.14 us  [local(): tiles_2 = lax.all_to_all(tiles_2, 'tensor', split_axis=0, concat_axis=0)]
  transfers between devices with their start and end apart: 12 -> 11, of which waited for: 10 -> 10; matrix products, arithmetic and copies ran while one was open for 12% -> 8% of each run, Pallas kernels for 0% -> 0%
where the time goes in v1:
time: 295 us; the launch traced here: 294 us
  waiting for transfers between devices  162 us (55%)
  starting transfers between devices  46.8 us (16%)
  blocking collectives  32.9 us (11%)
  matrix products  20 us (7%)
  between operations  14.3 us (5%)
  local copies, waits for them, and re-layouts  11.7 us (4%)
  other arithmetic  5.62 us (2%)
    all_to_all x5, waiting for transfers between devices, summed_on_arrival(): tiles = lax.all_to_all(split_up(shard, dim, size), axis, 0, 0, tiled=True)  73.8 us
    all_to_all x1, waiting for transfers between devices, local(): tiles_2 = lax.all_to_all(tiles_2, 'tensor', split_axis=0, concat_axis=0)  46.6 us
    all_to_all x4, waiting for transfers between devices, from_everyone(): lax.all_to_all(jnp.broadcast_to(shard[None], (size, *shard.shape)), axis,...  41.8 us
    all_to_all x1, blocking collectives, from_everyone(): lax.all_to_all(jnp.broadcast_to(shard[None], (size, *shard.shape)), axis,...  32.9 us
    all_to_all x5, starting transfers between devices, summed_on_arrival(): tiles = lax.all_to_all(split_up(shard, dim, size), axis, 0, 0, tiled=True)  25.8 us
    all_to_all x4, starting transfers between devices, from_everyone(): lax.all_to_all(jnp.broadcast_to(shard[None], (size, *shard.shape)), axis,...  16.9 us
  transfers between devices with their start and end apart: 11, of which 10 were waited for; matrix products, arithmetic and copies ran while one was open for 8% of the time, Pallas kernels for 0%

profile of v1, /device:TPU:8, one launch (start us, length us, event | category | flops | bytes accessed | tf_op | source)
XLA Modules:
  0.0 293.5 jit_solution(8180635275563733110)
XLA Ops:
  8.9 1.2 fusion.13
  10.1 32.9 %all_to_all.55 = f32[32,256,16]{1,2,0:T(8,128)S(1)} all-to-all(f32[32,256,16]{1,2,0:T(8,128)S(1)} %broadcast_in_dim.10), channel_id=1, replica_groups=mesh['dp'=16,'tensor'=32] {'tensor'}, dimensions={0} | all-to-all | bytes 1048576 | tf_op jit(solution)/shard_map/all_to_all | solution.py:12
  43.0 1.8 stack.2
  44.8 4.1 %all-to-all-start.2 = ((bf16[32,16,16,128]{3,2,1,0:T(8,128)(2,1)}), bf16[32,16,16,128]{3,2,1,0:T(8,128)(2,1)S(1)}, u32[]{:S(2)}, u32[]{:S(2)}) async-start(bf16[32,16,16,128]{3,2,1,0:T(8,128)(2,1)} %stack.2), calls=%async_computation.2 | async-start | bytes 4194304 | tf_op jit(solution)/shard_map/all_to_all | solution.py:87
  48.9 3.3 %fusion.9 = bf16[32,32,8,128]{3,2,1,0:T(8,128)(2,1)S(1)} fusion(bf16[256,448]{0,1:T(8,128)(2,1)S(1)} %copy-done.3, bf16[448,4096]{1,0:T(8,128)(2,1)} %param.8), kind=kOutput, calls=%fused_computation.11 | convolution fusion | flops 940572672 | bytes 5996544 | tf_op jit(solution)/shard_map/dot_general | solution.py:107
  52.3 1.9 copy.49
  54.2 46.6 %all-to-all-done.2 = bf16[32,16,16,128]{3,2,1,0:T(8,128)(2,1)S(1)} async-done(((bf16[32,16,16,128]{3,2,1,0:T(8,128)(2,1)}), bf16[32,16,16,128]{3,2,1,0:T(8,128)(2,1)S(1)}, u32[]{:S(2)}, u32[]{:S(2)}) %all-to-all-start.2) | async-done | bytes 2097184 | tf_op jit(solution)/shard_map/all_to_all | solution.py:87
  100.8 1.3 copy-done.1
  102.1 4.5 %all-to-all-start = ((bf16[32,256,128]{2,1,0:T(8,128)(2,1)}), bf16[32,256,128]{2,1,0:T(8,128)(2,1)S(1)}, u32[]{:S(2)}, u32[]{:S(2)}) async-start(bf16[32,256,128]{2,1,0:T(8,128)(2,1)} %bitcast.101), calls=%async_computation | async-start | bytes 4194304 | tf_op jit(solution)/shard_map/all_to_all | solution.py:29
  106.8 2.8 multiply_reduce_fusion
  109.7 4.4 %fusion.6 = f32[16,4096]{1,0:T(8,128)S(1)} fusion(bf16[448,4096]{1,0:T(8,128)(2,1)} %param.8, bf16[16,448,16]{1,2,0:T(8,128)(2,1)S(1)} %copy-done, bf16[32,16,16,128]{3,2,1,0:T(8,128)(2,1)} %copy-done.1), kind=kOutput, calls=%fused_computation.10 | convolution fusion | flops 942604288 | bytes 6258688 | tf_op jit(solution)/shard_map/dot_general | solution.py:92
  114.2 2.6 fusion.3
  117.7 40.8 %all-to-all-done = bf16[32,256,128]{2,1,0:T(8,128)(2,1)S(1)} async-done(((bf16[32,256,128]{2,1,0:T(8,128)(2,1)}), bf16[32,256,128]{2,1,0:T(8,128)(2,1)S(1)}, u32[]{:S(2)}, u32[]{:S(2)}) %all-to-all-start) | async-done | bytes 2097184 | tf_op jit(solution)/shard_map/all_to_all | solution.py:29
  158.5 4.5 %all-to-all-start.3 = ((bf16[32,16,128]{2,1,0:T(8,128)(2,1)}), bf16[32,16,128]{2,1,0:T(8,128)(2,1)S(1)}, u32[]{:S(2)}, u32[]{:S(2)}) async-start(bf16[32,16,128]{2,1,0:T(8,128)(2,1)} %copy.23), calls=%async_computation.3 | async-start | bytes 262144 | tf_op jit(solution)/shard_map/all_to_all | solution.py:29
  163.6 11.4 %all-to-all-done.3 = bf16[32,16,128]{2,1,0:T(8,128)(2,1)S(1)} async-done(((bf16[32,16,128]{2,1,0:T(8,128)(2,1)}), bf16[32,16,128]{2,1,0:T(8,128)(2,1)S(1)}, u32[]{:S(2)}, u32[]{:S(2)}) %all-to-all-start.3) | async-done | bytes 131104 | tf_op jit(solution)/shard_map/all_to_all | solution.py:29
  175.0 1.0 fusion.23
  176.9 7.6 %all-to-all-start.9 = ((bf16[16,1,128]{2,1,0:T(2,128)(2,1)}), bf16[16,1,128]{2,1,0:T(2,128)(2,1)S(1)}, u32[]{:S(2)}, u32[]{:S(2)}) async-start(bf16[16,1,128]{2,1,0:T(2,128)(2,1)} %copy.25), calls=%async_computation.9 | async-start | bytes 16384 | tf_op jit(solution)/shard_map/all_to_all | solution.py:29
  184.5 1.0 fusion.14
  185.5 6.0 %all-to-all-done.9 = bf16[16,1,128]{2,1,0:T(2,128)(2,1)S(1)} async-done(((bf16[16,1,128]{2,1,0:T(2,128)(2,1)}), bf16[16,1,128]{2,1,0:T(2,128)(2,1)S(1)}, u32[]{:S(2)}, u32[]{:S(2)}) %all-to-all-start.9) | async-done | bytes 4128 | tf_op jit(solution)/shard_map/all_to_all | solution.py:29
  192.4 3.9 %all-to-all-start.4 = ((f32[32,256,16]{1,2,0:T(8,128)}), f32[32,256,16]{1,2,0:T(8,128)S(1)}, u32[]{:S(2)}, u32[]{:S(2)}) async-start(f32[32,256,16]{1,2,0:T(8,128)} %broadcast_in_dim.11), calls=%async_computation.4 | async-start | bytes 1048576 | tf_op jit(solution)/shard_map/all_to_all | solution.py:12
  197.1 19.3 %all-to-all-done.4 = f32[32,256,16]{1,2,0:T(8,128)S(1)} async-done(((f32[32,256,16]{1,2,0:T(8,128)}), f32[32,256,16]{1,2,0:T(8,128)S(1)}, u32[]{:S(2)}, u32[]{:S(2)}) %all-to-all-start.4) | async-done | bytes 524320 | tf_op jit(solution)/shard_map/all_to_all | solution.py:12
  217.1 4.5 %all-to-all-start.10 = ((bf16[16,1,128]{2,1,0:T(2,128)(2,1)}), bf16[16,1,128]{2,1,0:T(2,128)(2,1)S(1)}, u32[]{:S(2)}, u32[]{:S(2)}) async-start(bf16[16,1,128]{2,1,0:T(2,128)(2,1)} %broadcast_in_dim.14), calls=%async_computation.10 | async-start | bytes 16384 | tf_op jit(solution)/shard_map/all_to_all | solution.py:12
  221.6 7.1 %all-to-all-done.10 = bf16[16,1,128]{2,1,0:T(2,128)(2,1)S(1)} async-done(((bf16[16,1,128]{2,1,0:T(2,128)(2,1)}), bf16[16,1,128]{2,1,0:T(2,128)(2,1)S(1)}, u32[]{:S(2)}, u32[]{:S(2)}) %all-to-all-start.10) | async-done | bytes 4128 | tf_op jit(solution)/shard_map/all_to_all | solution.py:12
  228.7 4.7 %all-to-all-start.7 = ((bf16[16,16,128]{2,1,0:T(8,128)(2,1)}), bf16[16,16,128]{2,1,0:T(8,128)(2,1)S(1)}, u32[]{:S(2)}, u32[]{:S(2)}) async-start(bf16[16,16,128]{2,1,0:T(8,128)(2,1)} %convolution_convert_fusion.2), calls=%async_computation.7 | async-start | bytes 131072 | tf_op jit(solution)/shard_map/all_to_all | solution.py:29
  234.5 6.6 %all-to-all-done.7 = bf16[16,16,128]{2,1,0:T(8,128)(2,1)S(1)} async-done(((bf16[16,16,128]{2,1,0:T(8,128)(2,1)}), bf16[16,16,128]{2,1,0:T(8,128)(2,1)S(1)}, u32[]{:S(2)}, u32[]{:S(2)}) %all-to-all-start.7) | async-done | bytes 65568 | tf_op jit(solution)/shard_map/all_to_all | solution.py:29
  241.1 4.4 %all-to-all-start.5 = ((bf16[16,448,16]{1,2,0:T(8,128)(2,1)}), bf16[16,448,16]{1,2,0:T(8,128)(2,1)S(1)}, u32[]{:S(2)}, u32[]{:S(2)}) async-start(bf16[16,448,16]{1,2,0:T(8,128)(2,1)} %bitcast.20), calls=%async_computation.5 | async-start | bytes 524288 | tf_op jit(solution)/shard_map/all_to_all | solution.py:29
  245.5 9.1 %all-to-all-done.5 = bf16[16,448,16]{1,2,0:T(8,128)(2,1)S(1)} async-done(((bf16[16,448,16]{1,2,0:T(8,128)(2,1)}), bf16[16,448,16]{1,2,0:T(8,128)(2,1)S(1)}, u32[]{:S(2)}, u32[]{:S(2)}) %all-to-all-start.5) | async-done | bytes 229408 | tf_op jit(solution)/shard_map/all_to_all | solution.py:29
  255.2 4.2 %all-to-all-start.8 = ((bf16[16,16,128]{2,1,0:T(8,128)(2,1)}), bf16[16,16,128]{2,1,0:T(8,128)(2,1)S(1)}, u32[]{:S(2)}, u32[]{:S(2)}) async-start(bf16[16,16,128]{2,1,0:T(8,128)(2,1)} %broadcast_in_dim.13), calls=%async_computation.8 | async-start | bytes 131072 | tf_op jit(solution)/shard_map/all_to_all | solution.py:12
  259.4 7.6 %all-to-all-done.8 = bf16[16,16,128]{2,1,0:T(8,128)(2,1)S(1)} async-done(((bf16[16,16,128]{2,1,0:T(8,128)(2,1)}), bf16[16,16,128]{2,1,0:T(8,128)(2,1)S(1)}, u32[]{:S(2)}, u32[]{:S(2)}) %all-to-all-start.8) | async-done | bytes 65568 | tf_op jit(solution)/shard_map/all_to_all | solution.py:12
  267.7 4.3 %all-to-all-start.6 = ((bf16[16,448,16]{1,2,0:T(8,128)(2,1)}), bf16[16,448,16]{1,2,0:T(8,128)(2,1)S(1)}, u32[]{:S(2)}, u32[]{:S(2)}) async-start(bf16[16,448,16]{1,2,0:T(8,128)(2,1)} %broadcast_in_dim.12), calls=%async_computation.6 | async-start | bytes 524288 | tf_op jit(solution)/shard_map/all_to_all | solution.py:12
  273.4 7.8 %all-to-all-done.6 = bf16[16,448,16]{1,2,0:T(8,128)(2,1)S(1)} async-done(((bf16[16,448,16]{1,2,0:T(8,128)(2,1)}), bf16[16,448,16]{1,2,0:T(8,128)(2,1)S(1)}, u32[]{:S(2)}, u32[]{:S(2)}) %all-to-all-start.6) | async-done | bytes 229408 | tf_op jit(solution)/shard_map/all_to_all | solution.py:12
  281.2 3.8 %fusion.45 = f32[256,448]{0,1:T(8,128)S(1)} fusion(bf16[256,4096]{1,0:T(8,128)(2,1)} %all-gather.2.cloned.1.call-done, bf16[448,4096]{1,0:T(8,128)(2,1)} %param.8), kind=kOutput, calls=%fused_computation.67 | convolution fusion | flops 939524096 | bytes 6225920 | tf_op jit(solution)/shard_map/dot_general | solution.py:130
  (56 shorter events, 12.2 us)
Async XLA Ops:
  7.2 1.7 copy-start
  7.2 35.8 %copy-start.6 = (bf16[16,16,128]{2,1,0:T(8,128)(2,1)S(1)}, bf16[16,16,128]{2,1,0:T(8,128)(2,1)}, u32[]{:S(2)}) copy-start(bf16[16,16,128]{2,1,0:T(8,128)(2,1)} %param.10) | copy-start | bytes 196612
  44.8 4.2 %copy-start.3 = (bf16[256,448]{0,1:T(8,128)(2,1)S(1)}, bf16[256,448]{0,1:T(8,128)(2,1)}, u32[]{:S(2)}) copy-start(bf16[256,448]{0,1:T(8,128)(2,1)} %param.7) | copy-start | bytes 688132
  44.8 56.0 %all-to-all-start.2 = ((bf16[32,16,16,128]{3,2,1,0:T(8,128)(2,1)}), bf16[32,16,16,128]{3,2,1,0:T(8,128)(2,1)S(1)}, u32[]{:S(2)}, u32[]{:S(2)}) async-start(bf16[32,16,16,128]{3,2,1,0:T(8,128)(2,1)} %stack.2), calls=%async_computation.2 | async-start | bytes 4194304 | tf_op jit(solution)/shard_map/all_to_all | solution.py:87
  100.8 1.3 copy-start.1
  102.1 56.4 %all-to-all-start = ((bf16[32,256,128]{2,1,0:T(8,128)(2,1)}), bf16[32,256,128]{2,1,0:T(8,128)(2,1)S(1)}, u32[]{:S(2)}, u32[]{:S(2)}) async-start(bf16[32,256,128]{2,1,0:T(8,128)(2,1)} %bitcast.101), calls=%async_computation | async-start | bytes 4194304 | tf_op jit(solution)/shard_map/all_to_all | solution.py:29
  109.7 4.5 %copy-start.2 = (bf16[32,16,16,128]{3,2,1,0:T(8,128)(2,1)S(1)}, bf16[32,16,16,128]{3,2,1,0:T(8,128)(2,1)}, u32[]{:S(2)}) copy-start(bf16[32,16,16,128]{3,2,1,0:T(8,128)(2,1)} %copy-done.1) | copy-start | bytes 6291460
  116.9 58.0 %copy-start.4 = (bf16[256,128]{1,0:T(8,128)(2,1)S(1)}, bf16[256,128]{1,0:T(8,128)(2,1)}, u32[]{:S(2)}) copy-start(bf16[256,128]{1,0:T(8,128)(2,1)} %param.13) | copy-start | bytes 196612
  117.0 58.0 %copy-start.7 = (bf16[16,128]{1,0:T(8,128)(2,1)S(1)}, bf16[16,128]{1,0:T(8,128)(2,1)}, u32[]{:S(2)}) copy-start(bf16[16,128]{1,0:T(8,128)(2,1)} %param.11) | copy-start | bytes 12292
  158.5 16.5 %all-to-all-start.3 = ((bf16[32,16,128]{2,1,0:T(8,128)(2,1)}), bf16[32,16,128]{2,1,0:T(8,128)(2,1)S(1)}, u32[]{:S(2)}, u32[]{:S(2)}) async-start(bf16[32,16,128]{2,1,0:T(8,128)(2,1)} %copy.23), calls=%async_computation.3 | async-start | bytes 262144 | tf_op jit(solution)/shard_map/all_to_all | solution.py:29
  163.0 118.2 %all-gather.2.cloned.1.call-start = ((), (), s32[]{:S(2)}) async-start(), calls=%async_computation.11 | async-start | bytes 2162688 | tf_op jit(solution)/shard_map/all_gather | solution.py:131
  176.0 20.3 %copy-start.5 = (bf16[256,128]{1,0:T(8,128)(2,1)S(1)}, bf16[256,128]{1,0:T(8,128)(2,1)}, u32[]{:S(2)}) copy-start(bf16[256,128]{1,0:T(8,128)(2,1)} %get-tuple-element.5) | copy-start | bytes 196612
  176.9 14.7 %all-to-all-start.9 = ((bf16[16,1,128]{2,1,0:T(2,128)(2,1)}), bf16[16,1,128]{2,1,0:T(2,128)(2,1)S(1)}, u32[]{:S(2)}, u32[]{:S(2)}) async-start(bf16[16,1,128]{2,1,0:T(2,128)(2,1)} %copy.25), calls=%async_computation.9 | async-start | bytes 16384 | tf_op jit(solution)/shard_map/all_to_all | solution.py:29
  192.4 24.1 %all-to-all-start.4 = ((f32[32,256,16]{1,2,0:T(8,128)}), f32[32,256,16]{1,2,0:T(8,128)S(1)}, u32[]{:S(2)}, u32[]{:S(2)}) async-start(f32[32,256,16]{1,2,0:T(8,128)} %broadcast_in_dim.11), calls=%async_computation.4 | async-start | bytes 1048576 | tf_op jit(solution)/shard_map/all_to_all | solution.py:12
  217.1 11.6 %all-to-all-start.10 = ((bf16[16,1,128]{2,1,0:T(2,128)(2,1)}), bf16[16,1,128]{2,1,0:T(2,128)(2,1)S(1)}, u32[]{:S(2)}, u32[]{:S(2)}) async-start(bf16[16,1,128]{2,1,0:T(2,128)(2,1)} %broadcast_in_dim.14), calls=%async_computation.10 | async-start | bytes 16384 | tf_op jit(solution)/shard_map/all_to_all | solution.py:12
  228.7 12.4 %all-to-all-start.7 = ((bf16[16,16,128]{2,1,0:T(8,128)(2,1)}), bf16[16,16,128]{2,1,0:T(8,128)(2,1)S(1)}, u32[]{:S(2)}, u32[]{:S(2)}) async-start(bf16[16,16,128]{2,1,0:T(8,128)(2,1)} %convolution_convert_fusion.2), calls=%async_computation.7 | async-start | bytes 131072 | tf_op jit(solution)/shard_map/all_to_all | solution.py:29
  241.1 13.5 %all-to-all-start.5 = ((bf16[16,448,16]{1,2,0:T(8,128)(2,1)}), bf16[16,448,16]{1,2,0:T(8,128)(2,1)S(1)}, u32[]{:S(2)}, u32[]{:S(2)}) async-start(bf16[16,448,16]{1,2,0:T(8,128)(2,1)} %bitcast.20), calls=%async_computation.5 | async-start | bytes 524288 | tf_op jit(solution)/shard_map/all_to_all | solution.py:29
  255.2 11.8 %all-to-all-start.8 = ((bf16[16,16,128]{2,1,0:T(8,128)(2,1)}), bf16[16,16,128]{2,1,0:T(8,128)(2,1)S(1)}, u32[]{:S(2)}, u32[]{:S(2)}) async-start(bf16[16,16,128]{2,1,0:T(8,128)(2,1)} %broadcast_in_dim.13), calls=%async_computation.8 | async-start | bytes 131072 | tf_op jit(solution)/shard_map/all_to_all | solution.py:12
  267.7 13.5 %all-to-all-start.6 = ((bf16[16,448,16]{1,2,0:T(8,128)(2,1)}), bf16[16,448,16]{1,2,0:T(8,128)(2,1)S(1)}, u32[]{:S(2)}, u32[]{:S(2)}) async-start(bf16[16,448,16]{1,2,0:T(8,128)(2,1)} %broadcast_in_dim.12), calls=%async_computation.6 | async-start | bytes 524288 | tf_op jit(solution)/shard_map/all_to_all | solution.py:12
Sparse Core Ops, SparseCore 0:
  176.2 80.3 all-gather.1
